TPU v7x, 32 devices: a whole 2x2x4 slice. The times are simulated.
32 devices in a mesh: chan: 4 (over z), ctx: 8 (over y, x, core).
Axes of the slice: x: 2, y: 2, z: 4, core: 2. Of those that a mesh axis runs over, the one named last changes fastest.
Arguments:
- queries: bfloat16 [8192, 1024], P('chan', 'ctx'), may hold values from -6 to 6
- keys: bfloat16 [8192, 1024], P('chan', 'ctx'), may hold values from -6 to 6
- values: bfloat16 [8192, 1024], P('chan', 'ctx'), may hold values from -6 to 6
- out_grad: bfloat16 [1024, 8192], P('ctx', 'chan'), may hold values from -6 to 6
- out_weight: bfloat16 [8192, 8192], P('chan'), may hold values from -0.0625 to 0.0625
- residues: float32 [16, 8192], P(None, 'chan'), may hold values from -1.5 to 1.5
- decay_rates: float32 [16, 8192], P(None, 'chan'), may hold values from 0.00048828125 to 1
Outputs:
- query_grad: bfloat16 [8192, 1024], P('chan', 'ctx')
- key_grad: bfloat16 [8192, 1024], P('chan', 'ctx')
- value_grad: bfloat16 [8192, 1024], P('chan', 'ctx')
- resid_grad: float32 [16, 8192], P(None, ('chan', 'ctx'))
- decay_grad: float32 [16, 8192], P(None, ('chan', 'ctx'))
All inputs are finite; a program needn't handle non-finite values.
Results may differ from a plain program's by a relative error of at most 0.0085.
Values may be sent and summed in bfloat16 or wider, within the bound.
A program may use at most 192 MiB of HBM per device.

v0:
```python
import math

import jax
import jax.numpy as jnp
from jax import lax
from jax.sharding import PartitionSpec as P

B = 1024


def dft_tables(block_size, section_size):
    total_size = section_size * block_size
    inner = jnp.arange(block_size, dtype=jnp.int32)
    outer = jnp.arange(section_size, dtype=jnp.int32)
    half_size = section_size // 2
    inner_angle = (inner[:, None] * inner[None, :] % block_size).astype(jnp.float32) * (
        2.0 * math.pi / block_size
    )
    twist_angle = (outer[:, None] * inner[None, :] % total_size).astype(jnp.float32) * (
        2.0 * math.pi / total_size
    )
    outer_rows = jnp.arange(half_size, dtype=jnp.int32)
    outer_angle = (outer_rows[:, None] * outer[None, :] % section_size).astype(jnp.float32) * (
        2.0 * math.pi / section_size
    )
    return (
        jnp.cos(inner_angle).astype(jnp.bfloat16),
        jnp.sin(inner_angle).astype(jnp.bfloat16),
        jnp.cos(twist_angle),
        jnp.sin(twist_angle),
        jnp.cos(outer_angle).astype(jnp.bfloat16),
        jnp.sin(outer_angle).astype(jnp.bfloat16),
    )


def forward(signal, tables):
    big_cos, big_sin, twist_cos, twist_sin, small_cos, small_sin = tables
    channels = signal.shape[0]
    half_size, section_size = small_cos.shape
    block_size = big_cos.shape[0]
    grid_view = signal.reshape(channels, half_size, block_size)
    real_part = jnp.einsum("chb,hk->ckb", grid_view, small_cos, preferred_element_type=jnp.float32)
    imag_part = -jnp.einsum("chb,hk->ckb", grid_view, small_sin, preferred_element_type=jnp.float32)
    turned_re = (
        (real_part * twist_cos + imag_part * twist_sin)
        .astype(jnp.bfloat16)
        .reshape(channels * section_size, block_size)
    )
    turned_im = (
        (imag_part * twist_cos - real_part * twist_sin)
        .astype(jnp.bfloat16)
        .reshape(channels * section_size, block_size)
    )
    out_re = jnp.dot(turned_re, big_cos, preferred_element_type=jnp.float32) + jnp.dot(
        turned_im, big_sin, preferred_element_type=jnp.float32
    )
    out_im = jnp.dot(turned_im, big_cos, preferred_element_type=jnp.float32) - jnp.dot(
        turned_re, big_sin, preferred_element_type=jnp.float32
    )
    return (
        out_re.reshape(channels, section_size, block_size),
        out_im.reshape(channels, section_size, block_size),
    )


def inverse(spec_re, spec_im, tables):
    big_cos, big_sin, twist_cos, twist_sin, small_cos, small_sin = tables
    channels, section_size, block_size = spec_re.shape
    half_size = small_cos.shape[0]
    flat_re = spec_re.astype(jnp.bfloat16).reshape(channels * section_size, block_size)
    flat_im = spec_im.astype(jnp.bfloat16).reshape(channels * section_size, block_size)
    back_re = jnp.dot(flat_re, big_cos, preferred_element_type=jnp.float32) - jnp.dot(
        flat_im, big_sin, preferred_element_type=jnp.float32
    )
    back_im = jnp.dot(flat_re, big_sin, preferred_element_type=jnp.float32) + jnp.dot(
        flat_im, big_cos, preferred_element_type=jnp.float32
    )
    back_re = back_re.reshape(channels, section_size, block_size)
    back_im = back_im.reshape(channels, section_size, block_size)
    wound_re = (back_re * twist_cos - back_im * twist_sin).astype(jnp.bfloat16)
    wound_im = (back_re * twist_sin + back_im * twist_cos).astype(jnp.bfloat16)
    grid_view = jnp.einsum(
        "ckb,hk->chb", wound_re, small_cos, preferred_element_type=jnp.float32
    ) - jnp.einsum("ckb,hk->chb", wound_im, small_sin, preferred_element_type=jnp.float32)
    return grid_view.reshape(channels, half_size * block_size) * (1.0 / (section_size * block_size))


def filter_spectrum(resid, rates, tables):
    small_cos = tables[4]
    section_size = small_cos.shape[1]
    block_size = tables[0].shape[0]
    total_size = section_size * block_size
    seq_length = total_size // 2
    frequency = (
        jnp.arange(section_size, dtype=jnp.int32)[:, None]
        + section_size * jnp.arange(block_size, dtype=jnp.int32)[None, :]
    )
    half_angle = frequency.astype(jnp.float32) * (math.pi / total_size)
    sine_half = jnp.sin(half_angle)
    sine_square = sine_half * sine_half
    sine_full = jnp.sin(2.0 * half_angle)
    parity = 1.0 - 2.0 * (frequency % 2).astype(jnp.float32)

    def add_mode(running, mode_vals):
        decay_rate, amplitude = mode_vals
        ratio = jnp.exp(-decay_rate)[:, None, None]
        one_minus = (-jnp.expm1(-decay_rate))[:, None, None]
        tail_value = jnp.exp(-decay_rate * seq_length)[:, None, None]
        root_gain = (amplitude * jnp.sqrt(2.0 * decay_rate))[:, None, None]
        den_real = one_minus + 2.0 * ratio * sine_square
        den_imag = ratio * sine_full
        modulus = one_minus * one_minus + 4.0 * ratio * sine_square
        numerator = root_gain * (1.0 - tail_value * parity) / modulus
        return ((running[0] + numerator * den_real, running[1] - numerator * den_imag), None)

    channels = resid.shape[1]
    initial = (
        jnp.zeros((channels, section_size, block_size), jnp.float32),
        jnp.zeros((channels, section_size, block_size), jnp.float32),
    )
    result, unused = lax.scan(add_mode, initial, (rates, resid))
    return result


def filter_grads(kernel_grad, resid, rates):
    positions = jnp.arange(kernel_grad.shape[1], dtype=jnp.int32).astype(jnp.float32)

    def one_mode(unused_carry, mode_vals):
        decay_rate, amplitude = mode_vals
        decay_curve = jnp.exp(-decay_rate[:, None] * positions[None, :])
        weighted = kernel_grad * decay_curve
        plain_sum = jnp.sum(weighted, axis=1)
        moment_sum = jnp.sum(weighted * positions[None, :], axis=1)
        root_gain = jnp.sqrt(2.0 * decay_rate)
        return (
            unused_carry,
            (
                root_gain * plain_sum,
                amplitude * root_gain * (0.5 * plain_sum - decay_rate * moment_sum),
            ),
        )

    unused, grads = lax.scan(one_mode, jnp.zeros((), jnp.float32), (rates, resid))
    return grads


def conv_forward(product, resid, rates, tables):
    spec_re, spec_im = filter_spectrum(resid, rates, tables)
    src_re, src_im = forward(product, tables)
    conv_out = inverse(
        spec_re * src_re - spec_im * src_im, spec_re * src_im + spec_im * src_re, tables
    ).astype(jnp.bfloat16)
    return (conv_out, (spec_re, spec_im, src_re, src_im))


def conv_backward(conv_grad, spectra, resid, rates, tables):
    spec_re, spec_im, src_re, src_im = spectra
    drv_re, drv_im = forward(conv_grad, tables)
    product_grad = inverse(
        spec_re * drv_re + spec_im * drv_im, spec_re * drv_im - spec_im * drv_re, tables
    ).astype(jnp.bfloat16)
    kernel_grad = inverse(
        drv_re * src_re + drv_im * src_im, drv_im * src_re - drv_re * src_im, tables
    )
    resid_grad, decay_grad = filter_grads(kernel_grad, resid, rates)
    return (product_grad, resid_grad, decay_grad)


def elementwise(left, right):
    return (left.astype(jnp.float32) * right.astype(jnp.float32)).astype(jnp.bfloat16)


def local(queries, keys, values, out_grad, out_weight, residues, decay_rates):
    channels, tokens = queries.shape
    ctx_size = lax.axis_size("ctx")
    group_width = channels // ctx_size
    seq_length = tokens * ctx_size
    section_size = 2 * seq_length // B
    tables = dft_tables(B, section_size)
    offset = lax.axis_index("ctx") * group_width
    resid = lax.dynamic_slice_in_dim(residues, offset, group_width, 1)
    rates = lax.dynamic_slice_in_dim(decay_rates, offset, group_width, 1)
    mixer_grad = jnp.einsum(
        "cd,td->ct",
        out_weight,
        lax.all_gather(out_grad, "chan", axis=1, tiled=True),
        preferred_element_type=jnp.float32,
    ).astype(jnp.bfloat16)
    query_cols, key_cols, value_cols, mixer_cols = (
        lax.all_to_all(queries, "ctx", split_axis=0, concat_axis=1, tiled=True),
        lax.all_to_all(keys, "ctx", split_axis=0, concat_axis=1, tiled=True),
        lax.all_to_all(values, "ctx", split_axis=0, concat_axis=1, tiled=True),
        lax.all_to_all(mixer_grad, "ctx", split_axis=0, concat_axis=1, tiled=True),
    )
    product = elementwise(key_cols, value_cols)
    conv_grad = elementwise(mixer_cols, query_cols)
    conv_out, spectra = conv_forward(product, resid, rates, tables)
    product_grad, resid_grad, decay_grad = conv_backward(conv_grad, spectra, resid, rates, tables)
    query_part = elementwise(mixer_cols, conv_out)
    key_part = elementwise(product_grad, value_cols)
    value_part = elementwise(product_grad, key_cols)
    query_grad, key_grad, value_grad = (
        lax.all_to_all(query_part, "ctx", split_axis=1, concat_axis=0, tiled=True),
        lax.all_to_all(key_part, "ctx", split_axis=1, concat_axis=0, tiled=True),
        lax.all_to_all(value_part, "ctx", split_axis=1, concat_axis=0, tiled=True),
    )
    return (query_grad, key_grad, value_grad, resid_grad, decay_grad)


def solution(mesh):
    placed = (
        P("chan", "ctx"),
        P("chan", "ctx"),
        P("chan", "ctx"),
        P("ctx", "chan"),
        P("chan", None),
        P(None, "chan"),
        P(None, "chan"),
    )
    return jax.shard_map(
        local,
        mesh=mesh,
        in_specs=placed,
        out_specs=(
            P("chan", "ctx"),
            P("chan", "ctx"),
            P("chan", "ctx"),
            P(None, ("chan", "ctx")),
            P(None, ("chan", "ctx")),
        ),
        check_vma=False,
    )
```

profile of v0, /device:TPU:0, one launch (start us, length us, event | category | flops | bytes accessed | tf_op | source)
XLA Modules:
  0.0 759.1 jit_solution(5223941057134443691)
XLA Ops:
  25.6 143.4 %while.31 = (s32[]{:T(128)}, f32[256,2,1024]{2,1,0:T(2,128)}, f32[256,2,1024]{2,1,0:T(2,128)S(1)}, f32[16,256]{1,0:T(8,128)S(1)}, f32[16,256]{1,0:T(8,128)S(1)}, /*index=5*/s32[1024]{0:T(1024)S(1)}, s32[]{:T(128)}, s32[]{:T(128)}) while((s32[]{:T(128)}, f32[256,2,1024]{2,1,0:T(2,128)}, ...), condition=%wide.region_1.2_spmd.clone.clone.clone.clone, body=%wide.region_0.1_spmd.clone.clone.clone.clone.sunk | while | flops 7905283 | bytes 8459371 | solution.py:121
  33.3 8.8 %select_subtract_fusion.2 = (f32[256,2,1024]{2,1,0:T(2,128)S(1)}, f32[256,2,1024]{2,1,0:T(2,128)}) fusion(f32[256,2,1024]{2,1,0:T(2,128)S(1)} %get-tuple-element.402, pred[]{:T(512)S(6)} %compare.13, f32[2,1024]{1,0:T(2,128)S(1)} %get-tuple-element.380, f32[256]{0:T(256)S(1)} %bitcast.121, f32[2,1024]{1,0:T(2,128)S(1)} %get-tuple-element.382, ...), kind=kLoop, calls=%fused_computation.13.clone.1 | loop fusion | flops 7864320 | bytes 8420353 | tf_op jit(solution)/shard_map/while/body/eval_jaxpr/sub | solution.py:114
  42.4 8.8 %select_subtract_fusion.2 = (f32[256,2,1024]{2,1,0:T(2,128)S(1)}, f32[256,2,1024]{2,1,0:T(2,128)}) fusion(f32[256,2,1024]{2,1,0:T(2,128)S(1)} %get-tuple-element.402, pred[]{:T(512)S(6)} %compare.13, f32[2,1024]{1,0:T(2,128)S(1)} %get-tuple-element.380, f32[256]{0:T(256)S(1)} %bitcast.121, f32[2,1024]{1,0:T(2,128)S(1)} %get-tuple-element.382, ...), kind=kLoop, calls=%fused_computation.13.clone.1 | loop fusion | flops 7864320 | bytes 8420353 | tf_op jit(solution)/shard_map/while/body/eval_jaxpr/sub | solution.py:114
  51.4 8.8 %select_subtract_fusion.2 = (f32[256,2,1024]{2,1,0:T(2,128)S(1)}, f32[256,2,1024]{2,1,0:T(2,128)}) fusion(f32[256,2,1024]{2,1,0:T(2,128)S(1)} %get-tuple-element.402, pred[]{:T(512)S(6)} %compare.13, f32[2,1024]{1,0:T(2,128)S(1)} %get-tuple-element.380, f32[256]{0:T(256)S(1)} %bitcast.121, f32[2,1024]{1,0:T(2,128)S(1)} %get-tuple-element.382, ...), kind=kLoop, calls=%fused_computation.13.clone.1 | loop fusion | flops 7864320 | bytes 8420353 | tf_op jit(solution)/shard_map/while/body/eval_jaxpr/sub | solution.py:114
  60.5 8.8 %select_subtract_fusion.2 = (f32[256,2,1024]{2,1,0:T(2,128)S(1)}, f32[256,2,1024]{2,1,0:T(2,128)}) fusion(f32[256,2,1024]{2,1,0:T(2,128)S(1)} %get-tuple-element.402, pred[]{:T(512)S(6)} %compare.13, f32[2,1024]{1,0:T(2,128)S(1)} %get-tuple-element.380, f32[256]{0:T(256)S(1)} %bitcast.121, f32[2,1024]{1,0:T(2,128)S(1)} %get-tuple-element.382, ...), kind=kLoop, calls=%fused_computation.13.clone.1 | loop fusion | flops 7864320 | bytes 8420353 | tf_op jit(solution)/shard_map/while/body/eval_jaxpr/sub | solution.py:114
  69.6 8.8 %select_subtract_fusion.2 = (f32[256,2,1024]{2,1,0:T(2,128)S(1)}, f32[256,2,1024]{2,1,0:T(2,128)}) fusion(f32[256,2,1024]{2,1,0:T(2,128)S(1)} %get-tuple-element.402, pred[]{:T(512)S(6)} %compare.13, f32[2,1024]{1,0:T(2,128)S(1)} %get-tuple-element.380, f32[256]{0:T(256)S(1)} %bitcast.121, f32[2,1024]{1,0:T(2,128)S(1)} %get-tuple-element.382, ...), kind=kLoop, calls=%fused_computation.13.clone.1 | loop fusion | flops 7864320 | bytes 8420353 | tf_op jit(solution)/shard_map/while/body/eval_jaxpr/sub | solution.py:114
  78.6 8.8 %select_subtract_fusion.2 = (f32[256,2,1024]{2,1,0:T(2,128)S(1)}, f32[256,2,1024]{2,1,0:T(2,128)}) fusion(f32[256,2,1024]{2,1,0:T(2,128)S(1)} %get-tuple-element.402, pred[]{:T(512)S(6)} %compare.13, f32[2,1024]{1,0:T(2,128)S(1)} %get-tuple-element.380, f32[256]{0:T(256)S(1)} %bitcast.121, f32[2,1024]{1,0:T(2,128)S(1)} %get-tuple-element.382, ...), kind=kLoop, calls=%fused_computation.13.clone.1 | loop fusion | flops 7864320 | bytes 8420353 | tf_op jit(solution)/shard_map/while/body/eval_jaxpr/sub | solution.py:114
  87.7 8.8 %select_subtract_fusion.2 = (f32[256,2,1024]{2,1,0:T(2,128)S(1)}, f32[256,2,1024]{2,1,0:T(2,128)}) fusion(f32[256,2,1024]{2,1,0:T(2,128)S(1)} %get-tuple-element.402, pred[]{:T(512)S(6)} %compare.13, f32[2,1024]{1,0:T(2,128)S(1)} %get-tuple-element.380, f32[256]{0:T(256)S(1)} %bitcast.121, f32[2,1024]{1,0:T(2,128)S(1)} %get-tuple-element.382, ...), kind=kLoop, calls=%fused_computation.13.clone.1 | loop fusion | flops 7864320 | bytes 8420353 | tf_op jit(solution)/shard_map/while/body/eval_jaxpr/sub | solution.py:114
  96.8 8.8 %select_subtract_fusion.2 = (f32[256,2,1024]{2,1,0:T(2,128)S(1)}, f32[256,2,1024]{2,1,0:T(2,128)}) fusion(f32[256,2,1024]{2,1,0:T(2,128)S(1)} %get-tuple-element.402, pred[]{:T(512)S(6)} %compare.13, f32[2,1024]{1,0:T(2,128)S(1)} %get-tuple-element.380, f32[256]{0:T(256)S(1)} %bitcast.121, f32[2,1024]{1,0:T(2,128)S(1)} %get-tuple-element.382, ...), kind=kLoop, calls=%fused_computation.13.clone.1 | loop fusion | flops 7864320 | bytes 8420353 | tf_op jit(solution)/shard_map/while/body/eval_jaxpr/sub | solution.py:114
  133.1 8.8 %select_subtract_fusion.2 = (f32[256,2,1024]{2,1,0:T(2,128)S(1)}, f32[256,2,1024]{2,1,0:T(2,128)}) fusion(f32[256,2,1024]{2,1,0:T(2,128)S(1)} %get-tuple-element.402, pred[]{:T(512)S(6)} %compare.13, f32[2,1024]{1,0:T(2,128)S(1)} %get-tuple-element.380, f32[256]{0:T(256)S(1)} %bitcast.121, f32[2,1024]{1,0:T(2,128)S(1)} %get-tuple-element.382, ...), kind=kLoop, calls=%fused_computation.13.clone.1 | loop fusion | flops 7864320 | bytes 8420353 | tf_op jit(solution)/shard_map/while/body/eval_jaxpr/sub | solution.py:114
  175.5 16.3 %convolution_convert_fusion = bf16[2048,128]{1,0:T(8,128)(2,1)} fusion(bf16[2048,8192]{1,0:T(8,128)(2,1)} %param.15, bf16[128,8192]{1,0:T(8,128)(2,1)} %all-gather.2.cloned.1.call-done), kind=kOutput, calls=%fused_computation.46 | convolution fusion | flops 4295229440 | bytes 36175872 | tf_op jit(solution)/shard_map/cd,td->ct/dot_general | solution.py:183
  229.0 17.5 %fusion.31 = f32[512,1024]{1,0:T(8,128)S(1)} fusion(bf16[512,1024]{1,0:T(8,128)(2,1)} %reshape.288), kind=kOutput, calls=%fused_computation.70 | convolution fusion | flops 1089470464 | bytes 3145728 | tf_op jit(solution)/shard_map/dot_general | solution.py:57
  246.6 16.5 %fusion.32 = f32[512,1024]{1,0:T(8,128)S(1)} fusion(bf16[512,1024]{1,0:T(8,128)(2,1)S(1)} %copy-done.18), kind=kOutput, calls=%fused_computation.71 | convolution fusion | flops 1089470464 | bytes 3145728 | tf_op jit(solution)/shard_map/dot_general | solution.py:54
  263.1 17.7 %fusion.44 = f32[512,1024]{1,0:T(8,128)} fusion(f32[512,1024]{1,0:T(8,128)S(1)} %fusion.31, bf16[512,1024]{1,0:T(8,128)(2,1)S(1)} %copy-done.18), kind=kOutput, calls=%fused_computation.84 | convolution fusion | flops 1089994752 | bytes 5242880 | tf_op jit(solution)/shard_map/dot_general | solution.py:57
  280.8 17.3 %fusion.43 = f32[512,1024]{1,0:T(8,128)} fusion(f32[512,1024]{1,0:T(8,128)S(1)} %fusion.32, bf16[512,1024]{1,0:T(8,128)(2,1)S(1)} %copy-done.19), kind=kOutput, calls=%fused_computation.83 | convolution fusion | flops 1089994752 | bytes 5242880 | tf_op jit(solution)/shard_map/dot_general | solution.py:54
  305.1 16.6 %fusion.28 = f32[512,1024]{1,0:T(8,128)S(1)} fusion(bf16[512,1024]{1,0:T(8,128)(2,1)S(1)} %copy-done.13), kind=kOutput, calls=%fused_computation.67 | convolution fusion | flops 1089470464 | bytes 3145728 | tf_op jit(solution)/shard_map/dot_general | solution.py:54
  321.8 17.2 %fusion.27 = f32[512,1024]{1,0:T(8,128)} fusion(bf16[512,1024]{1,0:T(8,128)(2,1)S(1)} %copy-done.14), kind=kOutput, calls=%fused_computation.66 | convolution fusion | flops 1089470464 | bytes 3145728 | tf_op jit(solution)/shard_map/dot_general | solution.py:57
  338.9 17.5 %fusion.47 = f32[512,1024]{1,0:T(8,128)} fusion(f32[512,1024]{1,0:T(8,128)S(1)} %fusion.28, bf16[512,1024]{1,0:T(8,128)(2,1)S(1)} %copy-done.14), kind=kOutput, calls=%fused_computation.87 | convolution fusion | flops 1089994752 | bytes 5242880 | tf_op jit(solution)/shard_map/dot_general | solution.py:54
  359.9 20.0 %add_convert_fusion.1 = (bf16[512,1024]{1,0:T(8,128)(2,1)}, bf16[512,1024]{1,0:T(8,128)(2,1)}, f32[512,1024]{1,0:T(8,128)}) fusion(f32[512,1024]{1,0:T(8,128)} %fusion.44, f32[512,1024]{1,0:T(8,128)} %fusion.47, f32[512,1024]{1,0:T(8,128)} %fusion.43, f32[512,1024]{1,0:T(8,128)} %fusion.27, bf16[512,1024]{1,0:T(8,128)(2,1)S(1)} %copy-done.13), kind=kOutput, calls=%fused_computation.50 | convolution fusion | flops 1094189056 | bytes 13631488 | tf_op jit(solution)/shard_map/dot_general | solution.py:57
  394.6 16.9 %fusion.30 = f32[512,1024]{1,0:T(8,128)S(1)} fusion(bf16[512,1024]{1,0:T(8,128)(2,1)S(1)} %reshape.291), kind=kOutput, calls=%fused_computation.69 | convolution fusion | flops 1089470464 | bytes 3145728 | tf_op jit(solution)/shard_map/dot_general | solution.py:72
  411.5 17.2 %fusion.29 = f32[512,1024]{1,0:T(8,128)} fusion(bf16[512,1024]{1,0:T(8,128)(2,1)S(1)} %reshape.292), kind=kOutput, calls=%fused_computation.68 | convolution fusion | flops 1089470464 | bytes 3145728 | tf_op jit(solution)/shard_map/dot_general | solution.py:75
  428.6 17.4 %fusion.45 = f32[512,1024]{1,0:T(8,128)} fusion(f32[512,1024]{1,0:T(8,128)S(1)} %fusion.30, bf16[512,1024]{1,0:T(8,128)(2,1)S(1)} %reshape.292), kind=kOutput, calls=%fused_computation.85 | convolution fusion | flops 1089994752 | bytes 5242880 | tf_op jit(solution)/shard_map/dot_general | solution.py:72
  448.6 19.4 %fusion.46 = f32[512,1024]{1,0:T(8,128)} fusion(f32[512,1024]{1,0:T(8,128)} %fusion.29, bf16[512,1024]{1,0:T(8,128)(2,1)} %copy-done.15), kind=kOutput, calls=%fused_computation.86 | convolution fusion | flops 1089994752 | bytes 5242880 | tf_op jit(solution)/shard_map/dot_general | solution.py:75
  481.0 16.5 %fusion.25 = f32[512,1024]{1,0:T(8,128)S(1)} fusion(bf16[512,1024]{1,0:T(8,128)(2,1)S(1)} %reshape.300), kind=kOutput, calls=%fused_computation.64 | convolution fusion | flops 1089470464 | bytes 3145728 | tf_op jit(solution)/shard_map/dot_general | solution.py:75
  497.5 17.1 %fusion.26 = f32[512,1024]{1,0:T(8,128)} fusion(bf16[512,1024]{1,0:T(8,128)(2,1)S(1)} %reshape.299), kind=kOutput, calls=%fused_computation.65 | convolution fusion | flops 1089470464 | bytes 3145728 | tf_op jit(solution)/shard_map/dot_general | solution.py:72
  514.6 17.7 %fusion.50 = f32[512,1024]{1,0:T(8,128)} fusion(f32[512,1024]{1,0:T(8,128)S(1)} %fusion.25, bf16[512,1024]{1,0:T(8,128)(2,1)S(1)} %reshape.299), kind=kOutput, calls=%fused_computation.90 | convolution fusion | flops 1089994752 | bytes 5242880 | tf_op jit(solution)/shard_map/dot_general | solution.py:75
  534.9 19.6 %fusion.49 = f32[512,1024]{1,0:T(8,128)} fusion(f32[512,1024]{1,0:T(8,128)} %fusion.26, bf16[512,1024]{1,0:T(8,128)(2,1)S(1)} %copy-done.17), kind=kOutput, calls=%fused_computation.89 | convolution fusion | flops 1089994752 | bytes 5242880 | tf_op jit(solution)/shard_map/dot_general | solution.py:72
  564.6 16.6 %fusion.24 = f32[512,1024]{1,0:T(8,128)S(1)} fusion(bf16[512,1024]{1,0:T(8,128)(2,1)S(1)} %copy-done.22), kind=kOutput, calls=%fused_computation.63 | convolution fusion | flops 1089470464 | bytes 3145728 | tf_op jit(solution)/shard_map/dot_general | solution.py:72
  581.2 16.5 %fusion.23 = f32[512,1024]{1,0:T(8,128)S(1)} fusion(bf16[512,1024]{1,0:T(8,128)(2,1)S(1)} %copy-done.23), kind=kOutput, calls=%fused_computation.62 | convolution fusion | flops 1089470464 | bytes 3145728 | tf_op jit(solution)/shard_map/dot_general | solution.py:75
  597.7 17.5 %fusion.51 = f32[512,1024]{1,0:T(8,128)} fusion(f32[512,1024]{1,0:T(8,128)S(1)} %fusion.24, bf16[512,1024]{1,0:T(8,128)(2,1)S(1)} %copy-done.23), kind=kOutput, calls=%fused_computation.91 | convolution fusion | flops 1089994752 | bytes 5242880 | tf_op jit(solution)/shard_map/dot_general | solution.py:72
  615.3 17.3 %fusion.52 = f32[512,1024]{1,0:T(8,128)} fusion(f32[512,1024]{1,0:T(8,128)S(1)} %fusion.23, bf16[512,1024]{1,0:T(8,128)(2,1)S(1)} %copy-done.22), kind=kOutput, calls=%fused_computation.92 | convolution fusion | flops 1089994752 | bytes 5242880 | tf_op jit(solution)/shard_map/dot_general | solution.py:75
  675.1 72.0 %while.30 = (s32[]{:T(128)}, f32[16,256]{1,0:T(8,128)}, f32[16,256]{1,0:T(8,128)}, f32[16,256]{1,0:T(8,128)}, f32[256,1024]{1,0:T(8,128)S(1)}, /*index=5*/f32[16,256]{1,0:T(8,128)}, s32[]{:T(128)}, s32[]{:T(128)}) while((s32[]{:T(128)}, f32[16,256]{1,0:T(8,128)}, f32[16,256]{1,0:T(8,128)}, f32[16,256]{1,0:T(8,128)}, ...), condition=%wide.region_5.6_spmd.clone.clone, body=%wide.region_2.5_spmd.clone.clone.sunk | while | flops 1313282 | bytes 1072237 | solution.py:143
  (276 shorter events, 298.2 us)
Async XLA Ops:
  7.2 14.9 %all-to-all-start.1 = ((bf16[8,256,128]{2,1,0:T(8,128)(2,1)}), bf16[8,256,128]{2,1,0:T(8,128)(2,1)S(1)}, u32[]{:S(2)}, u32[]{:S(2)}) async-start(bf16[8,256,128]{2,1,0:T(8,128)(2,1)} %bitcast.115), calls=%async_computation.1 | async-start | bytes 1048576 | tf_op jit(solution)/shard_map/all_to_all | solution.py:191
  12.3 163.1 %all-gather.2.cloned.1.call-start = ((), (), s32[]{:S(2)}) async-start(), calls=%async_computation.7 | async-start | bytes 2621440 | tf_op jit(solution)/shard_map/all_gather | solution.py:186
  22.1 175.9 %copy-start = (bf16[8,256,128]{2,1,0:T(8,128)(2,1)}, bf16[8,256,128]{2,1,0:T(8,128)(2,1)S(1)}, u32[]{:S(2)}) copy-start(bf16[8,256,128]{2,1,0:T(8,128)(2,1)S(1)} %all-to-all-done.1) | copy-start | bytes 1572868
  22.1 149.2 %all-to-all-start.2 = ((bf16[8,256,128]{2,1,0:T(8,128)(2,1)}), bf16[8,256,128]{2,1,0:T(8,128)(2,1)S(1)}, u32[]{:S(2)}, u32[]{:S(2)}) async-start(bf16[8,256,128]{2,1,0:T(8,128)(2,1)} %bitcast.117), calls=%async_computation.2 | async-start | bytes 1048576 | tf_op jit(solution)/shard_map/all_to_all | solution.py:192
  169.0 22.8 %copy-start.20 = (f32[16,256]{1,0:T(8,128)}, f32[16,256]{1,0:T(8,128)S(1)}, u32[]{:S(2)}) copy-start(f32[16,256]{1,0:T(8,128)S(1)} %get-tuple-element.466) | copy-start | bytes 49156
  169.0 22.8 %copy-start.21 = (f32[16,256]{1,0:T(8,128)}, f32[16,256]{1,0:T(8,128)S(1)}, u32[]{:S(2)}) copy-start(f32[16,256]{1,0:T(8,128)S(1)} %get-tuple-element.467) | copy-start | bytes 49156
  171.3 26.8 %copy-start.2 = (bf16[8,256,128]{2,1,0:T(8,128)(2,1)}, bf16[8,256,128]{2,1,0:T(8,128)(2,1)S(1)}, u32[]{:S(2)}) copy-start(bf16[8,256,128]{2,1,0:T(8,128)(2,1)S(1)} %all-to-all-done.2) | copy-start | bytes 1572868
  171.3 22.6 %all-to-all-start.4 = ((bf16[8,256,128]{1,2,0:T(8,128)(2,1)}), bf16[8,256,128]{1,2,0:T(8,128)(2,1)}, u32[]{:S(2)}, u32[]{:S(2)}) async-start(bf16[8,256,128]{1,2,0:T(8,128)(2,1)} %copy.33), calls=%async_computation.4 | async-start | bytes 1048576 | tf_op jit(solution)/shard_map/all_to_all | solution.py:190
  193.9 14.0 %all-to-all-start = ((bf16[8,256,128]{1,2,0:T(8,128)(2,1)}), bf16[8,256,128]{1,2,0:T(8,128)(2,1)}, u32[]{:S(2)}, u32[]{:S(2)}) async-start(bf16[8,256,128]{1,2,0:T(8,128)(2,1)} %copy.28), calls=%async_computation | async-start | bytes 1048576 | tf_op jit(solution)/shard_map/all_to_all | solution.py:193
  229.0 17.5 %copy-start.18 = (bf16[512,1024]{1,0:T(8,128)(2,1)S(1)}, bf16[512,1024]{1,0:T(8,128)(2,1)}, u32[]{:S(2)}) copy-start(bf16[512,1024]{1,0:T(8,128)(2,1)} %reshape.287) | copy-start | bytes 3145732
  263.1 17.7 %copy-start.19 = (bf16[512,1024]{1,0:T(8,128)(2,1)S(1)}, bf16[512,1024]{1,0:T(8,128)(2,1)}, u32[]{:S(2)}) copy-start(bf16[512,1024]{1,0:T(8,128)(2,1)} %reshape.288) | copy-start | bytes 3145732
  298.1 7.0 copy-start.13
  305.1 16.7 %copy-start.14 = (bf16[512,1024]{1,0:T(8,128)(2,1)S(1)}, bf16[512,1024]{1,0:T(8,128)(2,1)}, u32[]{:S(2)}) copy-start(bf16[512,1024]{1,0:T(8,128)(2,1)} %reshape.296) | copy-start | bytes 3145732
  394.5 16.9 %copy-start.15 = (bf16[512,1024]{1,0:T(8,128)(2,1)}, bf16[512,1024]{1,0:T(8,128)(2,1)S(1)}, u32[]{:S(2)}) copy-start(bf16[512,1024]{1,0:T(8,128)(2,1)S(1)} %reshape.291) | copy-start | bytes 3145732
  448.6 23.1 %copy-start.7 = (f32[256,2,1024]{2,1,0:T(2,128)}, f32[256,2,1024]{2,1,0:T(2,128)S(1)}, u32[]{:S(2)}) copy-start(f32[256,2,1024]{2,1,0:T(2,128)S(1)} %reshape.293) | copy-start | bytes 6291460
  471.7 4.2 copy-start.8
  475.9 4.2 copy-start.4
  480.9 16.5 %copy-start.16 = (bf16[512,1024]{1,0:T(8,128)(2,1)}, bf16[512,1024]{1,0:T(8,128)(2,1)S(1)}, u32[]{:S(2)}) copy-start(bf16[512,1024]{1,0:T(8,128)(2,1)S(1)} %reshape.300) | copy-start | bytes 3145732
  532.3 2.6 copy-start.17
  557.9 4.2 copy-start.9
  562.1 2.5 copy-start.22
  564.6 16.7 %copy-start.23 = (bf16[512,1024]{1,0:T(8,128)(2,1)S(1)}, bf16[512,1024]{1,0:T(8,128)(2,1)}, u32[]{:S(2)}) copy-start(bf16[512,1024]{1,0:T(8,128)(2,1)} %get-tuple-element.266) | copy-start | bytes 3145732
  615.2 17.3 %copy-start.11 = (f32[1,256,1024]{2,0,1:T(1,128)S(1)}, f32[1,256,1024]{2,0,1:T(1,128)}, u32[]{:S(2)}) copy-start(f32[1,256,1024]{2,0,1:T(1,128)} %fusion.66) | copy-start | bytes 3145732
  615.2 18.2 %copy-start.10 = (f32[1,256,1024]{2,0,1:T(1,128)S(1)}, f32[1,256,1024]{2,0,1:T(1,128)}, u32[]{:S(2)}) copy-start(f32[1,256,1024]{2,0,1:T(1,128)} %fusion.67) | copy-start | bytes 3145732
  634.4 6.6 copy-start.12
  636.7 20.9 %all-to-all-start.3 = ((bf16[256,8,128]{0,2,1:T(8,128)(2,1)}), bf16[256,8,128]{0,2,1:T(8,128)(2,1)}, u32[]{:S(2)}, u32[]{:S(2)}) async-start(bf16[256,8,128]{0,2,1:T(8,128)(2,1)} %fusion.59), calls=%async_computation.3 | async-start | bytes 1048576 | tf_op jit(solution)/shard_map/all_to_all | solution.py:203
  641.1 5.5 copy-start.1
  641.1 5.5 copy-start.3
  647.9 3.6 copy-start.5
  653.7 8.0 %copy-start.6 = (f32[256,2,1024]{2,1,0:T(2,128)S(1)}, f32[256,2,1024]{2,1,0:T(2,128)}, u32[]{:S(2)}) copy-start(f32[256,2,1024]{2,1,0:T(2,128)} %reshape.303) | copy-start | bytes 6291460
  657.6 14.0 %all-to-all-start.6 = ((bf16[256,8,128]{2,0,1:T(8,128)(2,1)}), bf16[256,8,128]{2,0,1:T(8,128)(2,1)}, u32[]{:S(2)}, u32[]{:S(2)}) async-start(bf16[256,8,128]{2,0,1:T(8,128)(2,1)} %get-tuple-element.277), calls=%async_computation.6 | async-start | bytes 1048576 | tf_op jit(solution)/shard_map/all_to_all | solution.py:205
  671.6 77.6 %all-to-all-start.5 = ((bf16[256,8,128]{2,0,1:T(8,128)(2,1)}), bf16[256,8,128]{2,0,1:T(8,128)(2,1)S(1)}, u32[]{:S(2)}, u32[]{:S(2)}) async-start(bf16[256,8,128]{2,0,1:T(8,128)(2,1)} %get-tuple-element.278), calls=%async_computation.5 | async-start | bytes 1048576 | tf_op jit(solution)/shard_map/all_to_all | solution.py:204
Sparse Core Ops, SparseCore 0:
  14.8 47.6 all-gather.1
where the time goes:
time: 774 us; the launch traced here: 759 us
  matrix products  389 us (50%)
  other arithmetic  197 us (25%)
  local copies, waits for them, and re-layouts  115 us (15%)
  starting transfers between devices  29.1 us (4%)
  between operations  15 us (2%)
  waiting for transfers between devices  13.2 us (2%)
    sub x16, other arithmetic, add_mode(): running[1] - numerator * den_imag  139 us
    dot_general x3, matrix products, inverse(): jnp.dot(flat_im, big_sin, preferred_element_type=jnp.float32)  54.5 us
    dot_general x3, matrix products, inverse(): jnp.dot(flat_re, big_sin, preferred_element_type=jnp.float32)  54.4 us
    dot_general x3, matrix products, inverse(): jnp.dot(flat_re, big_cos, preferred_element_type=jnp.float32)  50.7 us
    dot_general x3, matrix products, inverse(): jnp.dot(flat_im, big_cos, preferred_element_type=jnp.float32)  50.2 us
    dynamic_update_slice x32, local copies, waits for them, and re-layouts, filter_grads(): lax.scan(one_mode, jnp.zeros((), jnp.float32), (rates, resid))  41.9 us
    dot_general x2, matrix products, forward(): jnp.dot(turned_re, big_sin, preferred_element_type=jnp.float32)  37.8 us
    dot_general x2, matrix products, forward(): jnp.dot(turned_im, big_sin, preferred_element_type=jnp.float32)  34.8 us
  transfers between devices with their start and end apart: 8, of which 3 were waited for; matrix products, arithmetic and copies ran while one was open for 36% of the time, Pallas kernels for 0%

commit v1 on v0

v1 whole, which is shorter than its diff:
```python
import functools

import jax
import jax.numpy as jnp
from jax import lax
from jax.experimental import pallas as pl
from jax.experimental.pallas import tpu as pltpu
from jax.sharding import PartitionSpec as P

STEP = 16


def halves(width):
    lanes = min(width, 128)
    return [(start, lanes) for start in range(0, width, lanes)]


def fold_rows(rows):
    lanes = rows[0].shape[1]
    sub = lax.broadcasted_iota(jnp.int32, (8, lanes), 0)
    low4, low2, low1 = sub < 4, (sub & 2) == 0, (sub & 1) == 0
    four = []
    for i in range(4):
        a, b = rows[i], rows[i + 4]
        four.append(jnp.where(low4, a, b) + pltpu.roll(jnp.where(low4, b, a), 4, 0))
    two = []
    for i in range(2):
        a, b = four[i], four[i + 2]
        two.append(
            jnp.where(low2, a, pltpu.roll(b, 2, 0)) + jnp.where(low2, pltpu.roll(a, 6, 0), b)
        )
    a, b = two
    return jnp.where(low1, a, pltpu.roll(b, 1, 0)) + jnp.where(low1, pltpu.roll(a, 7, 0), b)


def mode_groups(rates_ref, resid_ref, start, lanes):
    groups = []
    for first in range(0, rates_ref.shape[0], 8):
        rate = rates_ref[pl.ds(first, 8), pl.ds(start, lanes)]
        gain = resid_ref[pl.ds(first, 8), pl.ds(start, lanes)] * jnp.sqrt(2.0 * rate)
        groups.append((jnp.exp(-rate), gain))
    return groups


def causal_scan(rates_ref, resid_ref, source_ref, out_ref):
    tokens, width = source_ref.shape
    columns = halves(width)
    modes = [mode_groups(rates_ref, resid_ref, *column) for column in columns]
    count = len(modes[0])

    def block(index, state):
        base = pl.multiple_of(index * STEP, STEP)
        state = [list(group) for group in state]
        for position, (start, lanes) in enumerate(columns):
            rows = source_ref[pl.ds(base, STEP), pl.ds(start, lanes)].astype(jnp.float32)
            sums = []
            for step in range(STEP):
                row = jnp.broadcast_to(rows[step : step + 1, :], (8, lanes))
                total = None
                for g in range(count):
                    decay, gain = modes[position][g]
                    held = decay * state[position][g] + row
                    state[position][g] = held
                    total = gain * held if total is None else total + gain * held
                sums.append(total)
            out_ref[pl.ds(base, STEP), pl.ds(start, lanes)] = jnp.concatenate(
                [fold_rows(sums[:8]), fold_rows(sums[8:])], axis=0
            ).astype(out_ref.dtype)
        return tuple(tuple(group) for group in state)

    zero = tuple(
        tuple(jnp.zeros((8, lanes), jnp.float32) for _ in range(count)) for _, lanes in columns
    )
    lax.fori_loop(0, tokens // STEP, block, zero)


def reverse_scan(
    rates_ref, resid_ref, source_ref, drive_ref, out_ref, resid_grad_ref, decay_grad_ref
):
    tokens, width = source_ref.shape
    columns = halves(width)
    modes = [mode_groups(rates_ref, resid_ref, *column) for column in columns]
    count = len(modes[0])
    blocks = tokens // STEP

    def block(index, state):
        base = pl.multiple_of((blocks - 1 - index) * STEP, STEP)
        state = [[list(item) for item in group] for group in state]
        for position, (start, lanes) in enumerate(columns):
            where = (pl.ds(base, STEP), pl.ds(start, lanes))
            source = source_ref[where].astype(jnp.float32)
            drive = drive_ref[where].astype(jnp.float32)
            sums = [None] * STEP
            for step in reversed(range(STEP)):
                source_row = jnp.broadcast_to(source[step : step + 1, :], (8, lanes))
                drive_row = jnp.broadcast_to(drive[step : step + 1, :], (8, lanes))
                total = None
                for g in range(count):
                    decay, gain = modes[position][g]
                    held, moment, plain_sum, moment_sum = state[position][g]
                    moment = decay * (moment + held)
                    held = decay * held + drive_row
                    state[position][g] = [
                        held,
                        moment,
                        plain_sum + source_row * held,
                        moment_sum + source_row * moment,
                    ]
                    total = gain * held if total is None else total + gain * held
                sums[step] = total
            out_ref[where] = jnp.concatenate(
                [fold_rows(sums[:8]), fold_rows(sums[8:])], axis=0
            ).astype(out_ref.dtype)
        return tuple(tuple(tuple(item) for item in group) for group in state)

    zero = tuple(
        tuple((jnp.zeros((8, lanes), jnp.float32),) * 4 for _ in range(count))
        for _, lanes in columns
    )
    final = lax.fori_loop(0, blocks, block, zero)
    for position, (start, lanes) in enumerate(columns):
        for g in range(count):
            where = (pl.ds(8 * g, 8), pl.ds(start, lanes))
            rate, amplitude = rates_ref[where], resid_ref[where]
            root = jnp.sqrt(2.0 * rate)
            plain_sum, moment_sum = final[position][g][2:]
            resid_grad_ref[where] = root * plain_sum
            decay_grad_ref[where] = amplitude * root * (0.5 * plain_sum - rate * moment_sum)


def elementwise(left, right):
    return (left.astype(jnp.float32) * right.astype(jnp.float32)).astype(jnp.bfloat16)


def local(queries, keys, values, out_grad, out_weight, residues, decay_rates):
    channels, tokens = queries.shape
    ctx_size = lax.axis_size("ctx")
    width = channels // ctx_size
    seq_length = tokens * ctx_size
    order = residues.shape[0]
    offset = lax.axis_index("ctx") * width
    resid = lax.dynamic_slice_in_dim(residues, offset, width, 1)
    rates = lax.dynamic_slice_in_dim(decay_rates, offset, width, 1)
    gathered = lax.all_gather(out_grad, "chan", axis=1, tiled=True)
    product = lax.all_to_all(
        elementwise(keys, values).T, "ctx", split_axis=1, concat_axis=0, tiled=True
    )
    sequence = jax.ShapeDtypeStruct((seq_length, width), jnp.bfloat16)
    grads = jax.ShapeDtypeStruct((order, width), jnp.float32)
    cost = pl.CostEstimate(
        flops=10 * order * seq_length * width, bytes_accessed=4 * seq_length * width, transcendentals=0
    )
    conv_out = pl.pallas_call(causal_scan, out_shape=sequence, cost_estimate=cost)(
        rates, resid, product
    )
    conv_out = lax.all_to_all(conv_out, "ctx", split_axis=0, concat_axis=1, tiled=True)
    mixer_grad = jnp.einsum(
        "cd,td->ct", out_weight, gathered, preferred_element_type=jnp.float32
    ).astype(jnp.bfloat16)
    conv_grad = lax.all_to_all(
        elementwise(mixer_grad, queries).T, "ctx", split_axis=1, concat_axis=0, tiled=True
    )
    product_grad, resid_grad, decay_grad = pl.pallas_call(
        reverse_scan, out_shape=(sequence, grads, grads), cost_estimate=cost
    )(rates, resid, product, conv_grad)
    product_grad = lax.all_to_all(product_grad, "ctx", split_axis=0, concat_axis=1, tiled=True).T
    return (
        elementwise(mixer_grad, conv_out.T),
        elementwise(product_grad, values),
        elementwise(product_grad, keys),
        resid_grad,
        decay_grad,
    )


def solution(mesh):
    placed = (
        P("chan", "ctx"),
        P("chan", "ctx"),
        P("chan", "ctx"),
        P("ctx", "chan"),
        P("chan", None),
        P(None, "chan"),
        P(None, "chan"),
    )
    return jax.shard_map(
        local,
        mesh=mesh,
        in_specs=placed,
        out_specs=(
            P("chan", "ctx"),
            P("chan", "ctx"),
            P("chan", "ctx"),
            P(None, ("chan", "ctx")),
            P(None, ("chan", "ctx")),
        ),
        check_vma=False,
    )
```

time: 774 us -> 120 us (0.16); the launches traced: 759 us -> 119 us
  matrix products: 389 us -> 16.5 us
  other arithmetic: 197 us -> 2.69 us
  local copies, waits for them, and re-layouts: 115 us -> 4.01 us
  blocking collectives: 0 us -> 39.6 us
  starting transfers between devices: 29.1 us -> 5.21 us
  Pallas kernels: 0 us -> 15.7 us
  waiting for transfers between devices: 13.2 us -> 21.7 us
    dot_general x27 -> x1, matrix products: 389 us -> 16.5 us  [local(): jnp.einsum('cd,td->ct', out_weight, gathered, preferred_element_type=jnp....]
    sub x16 -> x0, other arithmetic: 139 us -> none  [add_mode(): running[1] - numerator * den_imag]
    reshape x18 -> x0, local copies, waits for them, and re-layouts: 43.9 us -> none  [the longest x3 9.53 us: inverse(): back_re = back_re.reshape(channels, section_size, block_size)]
    dynamic_update_slice x32 -> x0, local copies, waits for them, and re-layouts: 41.9 us -> none  [filter_grads(): lax.scan(one_mode, jnp.zeros((), jnp.float32), (rates, resid))]
    all_to_all x0 -> x3, blocking collectives: none -> 39.6 us  [the longest x1 13.3 us: local(): lax.all_to_all(elementwise(mixer_grad, queries).T, 'ctx', split_axis=1, c...]
    all_to_all x7 -> x1, starting transfers between devices: 29 us -> 5.17 us  [local(): lax.all_to_all(elementwise(keys, values).T, 'ctx', split_axis=1, concat_a...]
    convert_element_type x20 -> x2, other arithmetic: 16.1 us -> 0.18 us  [the longest x1 0.09 us: elementwise(): right.astype(jnp.float32)]
    pallas_call x0 -> x2, Pallas kernels: none -> 15.7 us  [the longest x1 9.59 us: local(): pl.pallas_call(reverse_scan, out_shape=(sequence, grads, grads), cost_est...]
  transfers between devices with their start and end apart: 8 -> 2, of which waited for: 3 -> 2; matrix products, arithmetic and copies ran while one was open for 36% -> 3% of each run, Pallas kernels for 0% -> 5%
where the time goes in v1:
time: 120 us; the launch traced here: 119 us
  blocking collectives  39.6 us (33%)
  waiting for transfers between devices  21.7 us (18%)
  matrix products  16.5 us (14%)
  Pallas kernels  15.7 us (13%)
  between operations  14.1 us (12%)
  starting transfers between devices  5.21 us (4%)
  local copies, waits for them, and re-layouts  4.01 us (3%)
  other arithmetic  2.69 us (2%)
    dot_general x1, matrix products, local(): jnp.einsum('cd,td->ct', out_weight, gathered, preferred_element_type=jnp....  16.5 us
    all_to_all x1, blocking collectives, local(): lax.all_to_all(elementwise(mixer_grad, queries).T, 'ctx', split_axis=1, c...  13.3 us
    all_to_all x1, blocking collectives, local(): lax.all_to_all(conv_out, 'ctx', split_axis=0, concat_axis=1, tiled=True)  13.1 us
    all_to_all x1, blocking collectives, local(): lax.all_to_all(product_grad, 'ctx', split_axis=0, concat_axis=1, tiled=True)  13.1 us
    all_gather x1, waiting for transfers between devices, local(): gathered = lax.all_gather(out_grad, 'chan', axis=1, tiled=True)  12.6 us
    pallas_call x1, Pallas kernels, local(): pl.pallas_call(reverse_scan, out_shape=(sequence, grads, grads), cost_est...  9.59 us
    all_to_all x1, waiting for transfers between devices, local(): lax.all_to_all(elementwise(keys, values).T, 'ctx', split_axis=1, concat_a...  8.41 us
    pallas_call x1, Pallas kernels, local(): pl.pallas_call(causal_scan, out_shape=sequence, cost_estimate=cost)  6.06 us
  transfers between devices with their start and end apart: 2, of which 2 were waited for; matrix products, arithmetic and copies ran while one was open for 3% of the time, Pallas kernels for 5%

profile of v1, /device:TPU:0, one launch (start us, length us, event | category | flops | bytes accessed | tf_op | source)
XLA Modules:
  0.0 119.4 jit_solution(14506427186237221384)
XLA Ops:
  7.2 0.0 copy-start.1
  7.2 0.0 copy-start.2
  7.2 0.0 all-gather.2.cloned.1.call-start
  7.2 0.7 all-gather.2.cloned.1.call-update
  7.9 1.3 %fusion.2 = bf16[2048,128]{1,0:T(8,128)(2,1)S(1)} fusion(bf16[2048,128]{1,0:T(8,128)(2,1)} %param.9, bf16[2048,128]{1,0:T(8,128)(2,1)} %param.8), kind=kLoop, calls=%fused_computation.6 | loop fusion | flops 1048576 | bytes 1572864 | tf_op jit(solution)/shard_map/convert_element_type | solution.py:132
  9.3 1.0 copy.12
  10.3 5.2 %all-to-all-start = ((bf16[128,8,256]{2,0,1:T(8,128)(2,1)}), bf16[128,8,256]{2,0,1:T(8,128)(2,1)S(1)}, u32[]{:S(2)}, u32[]{:S(2)}) async-start(bf16[128,8,256]{2,0,1:T(8,128)(2,1)} %copy.12), calls=%async_computation | async-start | bytes 1048576 | tf_op jit(solution)/shard_map/all_to_all | solution.py:145
  15.4 1.3 %constant_dynamic-slice_fusion = (f32[16,256]{1,0:T(8,128)}, f32[16,256]{1,0:T(8,128)}) fusion(f32[16,2048]{1,0:T(8,128)} %param.12, s32[]{:T(128)S(6)} %select_n.4, f32[16,2048]{1,0:T(8,128)} %param.13), kind=kLoop, calls=%fused_computation.13 | loop fusion | bytes 65540 | tf_op jit(solution)/shard_map/dynamic_slice | solution.py:142
  16.8 8.4 %all-to-all-done = bf16[128,8,256]{2,0,1:T(8,128)(2,1)S(1)} async-done(((bf16[128,8,256]{2,0,1:T(8,128)(2,1)}), bf16[128,8,256]{2,0,1:T(8,128)(2,1)S(1)}, u32[]{:S(2)}, u32[]{:S(2)}) %all-to-all-start) | async-done | bytes 524320 | tf_op jit(solution)/shard_map/all_to_all | solution.py:145
  25.2 0.0 copy-start
  25.2 0.8 copy-done
  26.0 6.1 %shard_map.110 = bf16[1024,256]{1,0:T(8,128)(2,1)} custom-call(f32[16,256]{1,0:T(8,128)} %get-tuple-element.16.rates_ref, f32[16,256]{1,0:T(8,128)} %get-tuple-element.15.resid_ref, bf16[1024,256]{1,0:T(8,128)(2,1)} %bitcast.31), custom_call_target="tpu_custom_call" | custom-call | flops 41943040 | bytes 1048576 | tf_op jit(solution)/shard_map/pallas_call | solution.py:153
  32.0 13.1 %all_to_all.64 = bf16[8,128,256]{2,1,0:T(8,128)(2,1)S(1)} all-to-all(bf16[8,128,256]{2,1,0:T(8,128)(2,1)} %bitcast.35), channel_id=1, replica_groups=mesh['chan'=4,'ctx'=8] {'ctx'}, dimensions={0} | all-to-all | bytes 1048576 | tf_op jit(solution)/shard_map/all_to_all | solution.py:156
  45.2 0.1 convert_bitcast_fusion.1
  45.3 0.3 copy.13
  45.6 12.6 %all-gather.2.cloned.1.call-done = bf16[128,8192]{1,0:T(8,128)(2,1)} async-done(((bf16[128,2048]{1,0:T(8,128)(2,1)}), bf16[128,8192]{1,0:T(8,128)(2,1)}) %all-gather.2.cloned.1.call-update) | async-done | bytes 2097168 | tf_op jit(solution)/shard_map/all_gather | solution.py:144
  58.3 16.5 %multiply_convert_fusion = (bf16[2048,128]{1,0:T(8,128)(2,1)S(1)}, bf16[2048,128]{1,0:T(8,128)(2,1)}) fusion(bf16[2048,128]{1,0:T(8,128)(2,1)} %param.7, f32[128,8,256]{0,2,1:T(8,128)S(1)} %copy.13, bf16[2048,8192]{1,0:T(8,128)(2,1)} %param.11, bf16[128,8192]{1,0:T(8,128)(2,1)} %all-gather.2.cloned.1.call-done), kind=kOutput, calls=%fused_computation.12 | convolution fusion | flops 4296802304 | bytes 38273024 | tf_op jit(solution)/shard_map/cd,td->ct/dot_general | solution.py:157
  74.7 0.2 copy.14
  74.9 13.3 %all_to_all.65 = bf16[128,8,256]{2,0,1:T(8,128)(2,1)} all-to-all(bf16[128,8,256]{2,0,1:T(8,128)(2,1)S(1)} %copy.14), channel_id=1, replica_groups=mesh['chan'=4,'ctx'=8] {'ctx'}, dimensions={1} | all-to-all | bytes 1048576 | tf_op jit(solution)/shard_map/all_to_all | solution.py:160
  88.2 9.6 %shard_map.111 = (bf16[1024,256]{1,0:T(8,128)(2,1)}, f32[16,256]{1,0:T(8,128)}, f32[16,256]{1,0:T(8,128)}) custom-call(f32[16,256]{1,0:T(8,128)} %get-tuple-element.16.rates_ref, f32[16,256]{1,0:T(8,128)} %get-tuple-element.15.resid_ref, bf16[1024,256]{1,0:T(8,128)(2,1)} %bitcast.32, bf16[1024,256]{1,0:T(8,128)(2,1)} %bitcast.34), custom_call_target="tpu_custom_call" | custom-call | flops 41943040 | bytes 1048576 | tf_op jit(solution)/shard_map/pallas_call | solution.py:163
  97.8 13.1 %all_to_all.66 = bf16[8,128,256]{2,1,0:T(8,128)(2,1)S(1)} all-to-all(bf16[8,128,256]{2,1,0:T(8,128)(2,1)} %bitcast.36), channel_id=1, replica_groups=mesh['chan'=4,'ctx'=8] {'ctx'}, dimensions={0} | all-to-all | bytes 1048576 | tf_op jit(solution)/shard_map/all_to_all | solution.py:166
  111.0 0.1 convert_bitcast_fusion
  111.0 0.3 copy.15
  111.4 0.0 copy-done.1
  111.4 0.0 copy-done.2
  111.4 1.2 fusion.1
Async XLA Ops:
  7.2 104.2 %copy-start.1 = (bf16[2048,128]{1,0:T(8,128)(2,1)S(1)}, bf16[2048,128]{1,0:T(8,128)(2,1)}, u32[]{:S(2)}) copy-start(bf16[2048,128]{1,0:T(8,128)(2,1)} %param.9) | copy-start | bytes 1572868
  7.2 104.2 %copy-start.2 = (bf16[2048,128]{1,0:T(8,128)(2,1)S(1)}, bf16[2048,128]{1,0:T(8,128)(2,1)}, u32[]{:S(2)}) copy-start(bf16[2048,128]{1,0:T(8,128)(2,1)} %param.8) | copy-start | bytes 1572868
  7.2 51.1 %all-gather.2.cloned.1.call-start = ((), (), s32[]{:S(2)}) async-start(), calls=%async_computation.4 | async-start | bytes 2621440 | tf_op jit(solution)/shard_map/all_gather | solution.py:144
  10.3 14.9 %all-to-all-start = ((bf16[128,8,256]{2,0,1:T(8,128)(2,1)}), bf16[128,8,256]{2,0,1:T(8,128)(2,1)S(1)}, u32[]{:S(2)}, u32[]{:S(2)}) async-start(bf16[128,8,256]{2,0,1:T(8,128)(2,1)} %copy.12), calls=%async_computation | async-start | bytes 1048576 | tf_op jit(solution)/shard_map/all_to_all | solution.py:145
  25.2 0.8 copy-start
Sparse Core Ops, SparseCore 0:
  9.6 48.6 all-gather.1

commit v2 on v1

v2 whole, which is shorter than its diff:
```python
import functools

import jax
import jax.numpy as jnp
from jax import lax
from jax.experimental import pallas as pl
from jax.experimental.pallas import tpu as pltpu
from jax.sharding import PartitionSpec as P

STEP = 16


def halves(width):
    lanes = min(width, 128)
    return [(start, lanes) for start in range(0, width, lanes)]


def fold_rows(rows):
    lanes = rows[0].shape[1]
    sub = lax.broadcasted_iota(jnp.int32, (8, lanes), 0)
    low4, low2, low1 = sub < 4, (sub & 2) == 0, (sub & 1) == 0
    four = []
    for i in range(4):
        a, b = rows[i], rows[i + 4]
        four.append(jnp.where(low4, a, b) + pltpu.roll(jnp.where(low4, b, a), 4, 0))
    two = []
    for i in range(2):
        a, b = four[i], four[i + 2]
        two.append(
            jnp.where(low2, a, pltpu.roll(b, 2, 0)) + jnp.where(low2, pltpu.roll(a, 6, 0), b)
        )
    a, b = two
    return jnp.where(low1, a, pltpu.roll(b, 1, 0)) + jnp.where(low1, pltpu.roll(a, 7, 0), b)


def axis_device(axis, index):
    return {axis: index}


def exchange(outgoing, incoming, sends, arrivals, me, other):
    return pltpu.make_async_remote_copy(
        src_ref=outgoing.at[other],
        dst_ref=incoming.at[me],
        send_sem=sends.at[other],
        recv_sem=arrivals.at[me],
        device_id=axis_device("ctx", other),
        device_id_type=pl.DeviceIdType.MESH,
    )


def expect(outgoing, incoming, sends, arrivals, other):
    return pltpu.make_async_remote_copy(
        src_ref=outgoing.at[other],
        dst_ref=incoming.at[other],
        send_sem=sends.at[other],
        recv_sem=arrivals.at[other],
        device_id=axis_device("ctx", other),
        device_id_type=pl.DeviceIdType.MESH,
    )


def body(
    chan_size,
    ctx_size,
    queries,
    keys,
    values,
    out_grad,
    out_weight,
    residues,
    decay_rates,
    query_grad,
    key_grad,
    value_grad,
    resid_grad,
    decay_grad,
    weight,
    gathered,
    mixer,
    product_out,
    product_in,
    conv_out_out,
    conv_out_in,
    conv_grad_out,
    conv_grad_in,
    product_grad_out,
    product_grad_in,
    weight_sems,
    shard_arrivals,
    up_sends,
    down_sends,
    sends,
    arrivals,
):
    place = lax.axis_index("chan")
    me = lax.axis_index("ctx")
    channels, tokens = queries.shape
    depth = out_grad.shape[1]
    width = channels // ctx_size
    order = residues.shape[0]
    columns = halves(width)
    count = order // 8
    blocks = tokens // STEP
    f32, bf16 = jnp.float32, jnp.bfloat16
    offset = pl.multiple_of(me * width, width) if residues.shape[1] != width else 0

    def links(kind, outgoing, incoming):
        return (outgoing, incoming, sends.at[kind], arrivals.at[kind])

    product_links = links(0, product_out, product_in)
    conv_out_links = links(1, conv_out_out, conv_out_in)
    conv_grad_links = links(2, conv_grad_out, conv_grad_in)
    product_grad_links = links(3, product_grad_out, product_grad_in)

    def send_or_keep(link, other):
        @pl.when(other != me)
        def _():
            exchange(*link, me, other).start()

        @pl.when(other == me)
        def _():
            link[1][me] = link[0][me]

    def await_slot(link, other):
        @pl.when(other != me)
        def _():
            expect(*link, other).wait_recv()

    def weight_copy(shard):
        return pltpu.make_async_copy(
            out_weight.at[:, pl.ds(pl.multiple_of(shard * depth, depth), depth)],
            weight.at[shard],
            weight_sems.at[shard],
        )

    def shard_copy(source, shard, going_up):
        return pltpu.make_async_remote_copy(
            src_ref=source,
            dst_ref=gathered.at[shard],
            send_sem=(up_sends if going_up else down_sends).at[shard],
            recv_sem=shard_arrivals.at[shard],
            device_id=axis_device("chan", place + 1 if going_up else place - 1),
            device_id_type=pl.DeviceIdType.MESH,
        )

    weight_copy(place).start()
    for distance in range(1, chan_size):
        for shard, present in (
            (place - distance, place >= distance),
            (place + distance, place + distance < chan_size),
        ):

            @pl.when(present)
            def _():
                weight_copy(shard).start()

    barrier = pltpu.get_barrier_semaphore()
    for step in range(1, ctx_size):
        pl.semaphore_signal(
            barrier,
            inc=1,
            device_id=axis_device("ctx", lax.rem(me + step, ctx_size)),
            device_id_type=pl.DeviceIdType.MESH,
        )
    for step in range(1, chan_size):
        pl.semaphore_signal(
            barrier,
            inc=1,
            device_id=axis_device("chan", lax.rem(place + step, chan_size)),
            device_id_type=pl.DeviceIdType.MESH,
        )
    pl.semaphore_wait(barrier, ctx_size + chan_size - 2)

    @pl.when(place < chan_size - 1)
    def _():
        shard_copy(out_grad, place, True).start()

    @pl.when(place > 0)
    def _():
        shard_copy(out_grad, place, False).start()

    @pl.loop(0, ctx_size)
    def _(step):
        other = lax.rem(me + 1 + step, ctx_size)
        rows = pl.ds(pl.multiple_of(other * width, width), width)
        pair = keys[rows, :].astype(f32) * values[rows, :].astype(f32)
        product_out[other] = pair.astype(bf16).astype(f32).T.astype(bf16)
        send_or_keep(product_links, other)

    tile = min(channels, 512)

    def multiply(source, shard, first):
        @pl.loop(0, channels // tile)
        def _(index):
            rows = pl.ds(pl.multiple_of(index * tile, tile), tile)
            term = lax.dot_general(
                weight[shard, rows, :],
                source[...],
                (((1,), (1,)), ((), ())),
                preferred_element_type=f32,
            )
            mixer[rows, :] = term if first else mixer[rows, :] + term

    weight_copy(place).wait()
    multiply(out_grad, place, True)

    def gather_step(distance):
        sides = (
            (place - distance, place >= distance, place < chan_size - 1, True),
            (place + distance, place + distance < chan_size, place > 0, False),
        )
        for shard, present, onward, going_up in sides:

            @pl.when(present)
            def _():
                shard_copy(gathered.at[shard], shard, going_up).wait_recv()

                @pl.when(onward)
                def _():
                    shard_copy(gathered.at[shard], shard, going_up).start()

        for shard, present, onward, going_up in sides:

            @pl.when(present)
            def _():
                weight_copy(shard).wait()
                multiply(gathered.at[shard], shard, False)

    def mode_groups(start, lanes):
        groups = []
        for g in range(count):
            where = (pl.ds(8 * g, 8), pl.ds(offset + start, lanes))
            rate = decay_rates[where]
            groups.append((jnp.exp(-rate), residues[where] * jnp.sqrt(2.0 * rate)))
        return groups

    def causal_scan():
        modes = [mode_groups(*column) for column in columns]

        def chunk(slot, state):
            await_slot(product_links, slot)

            def block(index, state):
                base = pl.multiple_of(index * STEP, STEP)
                state = [list(group) for group in state]
                for position, (start, lanes) in enumerate(columns):
                    where = (slot, pl.ds(base, STEP), pl.ds(start, lanes))
                    rows = product_in[where].astype(f32)
                    totals = []
                    for step in range(STEP):
                        row = jnp.broadcast_to(rows[step : step + 1, :], (8, lanes))
                        total = None
                        for g in range(count):
                            decay, gain = modes[position][g]
                            held = decay * state[position][g] + row
                            state[position][g] = held
                            total = gain * held if total is None else total + gain * held
                        totals.append(total)
                    conv_out_out[where] = jnp.concatenate(
                        [fold_rows(totals[:8]), fold_rows(totals[8:])], axis=0
                    ).astype(bf16)
                return tuple(tuple(group) for group in state)

            state = lax.fori_loop(0, blocks, block, state)
            send_or_keep(conv_out_links, slot)
            return state

        zero = tuple(
            tuple(jnp.zeros((8, lanes), f32) for _ in range(count)) for _, lanes in columns
        )
        lax.fori_loop(0, ctx_size, chunk, zero)

    def reverse_scan():
        modes = [mode_groups(*column) for column in columns]

        def chunk(step_index, state):
            slot = ctx_size - 1 - step_index
            await_slot(conv_grad_links, slot)

            def block(index, state):
                base = pl.multiple_of((blocks - 1 - index) * STEP, STEP)
                state = [[list(item) for item in group] for group in state]
                for position, (start, lanes) in enumerate(columns):
                    where = (slot, pl.ds(base, STEP), pl.ds(start, lanes))
                    source = product_in[where].astype(f32)
                    drive = conv_grad_in[where].astype(f32)
                    totals = [None] * STEP
                    for step in reversed(range(STEP)):
                        source_row = jnp.broadcast_to(source[step : step + 1, :], (8, lanes))
                        drive_row = jnp.broadcast_to(drive[step : step + 1, :], (8, lanes))
                        total = None
                        for g in range(count):
                            decay, gain = modes[position][g]
                            held, moment, plain_sum, moment_sum = state[position][g]
                            moment = decay * (moment + held)
                            held = decay * held + drive_row
                            state[position][g] = [
                                held,
                                moment,
                                plain_sum + source_row * held,
                                moment_sum + source_row * moment,
                            ]
                            total = gain * held if total is None else total + gain * held
                        totals[step] = total
                    product_grad_out[where] = jnp.concatenate(
                        [fold_rows(totals[:8]), fold_rows(totals[8:])], axis=0
                    ).astype(bf16)
                return tuple(tuple(tuple(item) for item in group) for group in state)

            state = lax.fori_loop(0, blocks, block, state)
            send_or_keep(product_grad_links, slot)
            return state

        zero = tuple(
            tuple((jnp.zeros((8, lanes), f32),) * 4 for _ in range(count)) for _, lanes in columns
        )
        final = lax.fori_loop(0, ctx_size, chunk, zero)
        for position, (start, lanes) in enumerate(columns):
            for g in range(count):
                where = (pl.ds(8 * g, 8), pl.ds(offset + start, lanes))
                rate, amplitude = decay_rates[where], residues[where]
                root = jnp.sqrt(2.0 * rate)
                plain_sum, moment_sum = final[position][g][2:]
                put = (pl.ds(8 * g, 8), pl.ds(start, lanes))
                resid_grad[put] = root * plain_sum
                decay_grad[put] = amplitude * root * (0.5 * plain_sum - rate * moment_sum)

    for distance in range(1, chan_size):
        gather_step(distance)
        if distance == 1:
            causal_scan()
    if chan_size == 1:
        causal_scan()

    @pl.loop(0, ctx_size)
    def _(step):
        other = lax.rem(me + 1 + step, ctx_size)
        rows = pl.ds(pl.multiple_of(other * width, width), width)
        pair = mixer[rows, :].astype(bf16).astype(f32) * queries[rows, :].astype(f32)
        conv_grad_out[other] = pair.astype(bf16).astype(f32).T.astype(bf16)
        send_or_keep(conv_grad_links, other)

    reverse_scan()

    @pl.loop(0, ctx_size)
    def _(slot):
        await_slot(conv_out_links, slot)
        rows = pl.ds(pl.multiple_of(slot * width, width), width)
        result = conv_out_in[slot].astype(f32).T
        query_grad[rows, :] = (mixer[rows, :].astype(bf16).astype(f32) * result).astype(bf16)

    @pl.loop(0, ctx_size)
    def _(slot):
        await_slot(product_grad_links, slot)
        rows = pl.ds(pl.multiple_of(slot * width, width), width)
        result = product_grad_in[slot].astype(f32).T
        key_grad[rows, :] = (result * values[rows, :].astype(f32)).astype(bf16)
        value_grad[rows, :] = (result * keys[rows, :].astype(f32)).astype(bf16)

    @pl.loop(0, ctx_size)
    def _(other):
        @pl.when(other != me)
        def _():
            for link in (product_links, conv_out_links, conv_grad_links, product_grad_links):
                exchange(*link, me, other).wait_send()

    for distance in range(chan_size):
        for shard, present, onward, going_up in (
            (place - distance, place >= distance, place < chan_size - 1, True),
            (place + distance, place + distance < chan_size, place > 0, False),
        ):

            @pl.when(present & onward)
            def _():
                source = out_grad if distance == 0 else gathered.at[shard]
                shard_copy(source, shard, going_up).wait_send()


def local(queries, keys, values, out_grad, out_weight, residues, decay_rates):
    channels, tokens = queries.shape
    chan_size = lax.axis_size("chan")
    ctx_size = lax.axis_size("ctx")
    width = channels // ctx_size
    depth = out_grad.shape[1]
    order = residues.shape[0]
    if width % 128:
        offset = lax.axis_index("ctx") * width
        residues = lax.dynamic_slice_in_dim(residues, offset, width, 1)
        decay_rates = lax.dynamic_slice_in_dim(decay_rates, offset, width, 1)
    gate = jax.ShapeDtypeStruct((channels, tokens), jnp.bfloat16)
    grads = jax.ShapeDtypeStruct((order, width), jnp.float32)
    vmem = pl.BlockSpec(memory_space=pltpu.VMEM)
    slots = pltpu.VMEM((ctx_size, tokens, width), jnp.bfloat16)
    dma = pltpu.SemaphoreType.DMA
    return tuple(
        pl.pallas_call(
            functools.partial(body, chan_size, ctx_size),
            out_shape=(gate, gate, gate, grads, grads),
            in_specs=[vmem, vmem, vmem, vmem, pl.BlockSpec(memory_space=pl.ANY), vmem, vmem],
            out_specs=(vmem,) * 5,
            scratch_shapes=[
                pltpu.VMEM((chan_size, channels, depth), jnp.bfloat16),
                pltpu.VMEM((chan_size, tokens, depth), jnp.bfloat16),
                pltpu.VMEM((channels, tokens), jnp.float32),
                *[slots] * 8,
                dma((chan_size,)),
                dma((chan_size,)),
                dma((chan_size,)),
                dma((chan_size,)),
                dma((4, ctx_size)),
                dma((4, ctx_size)),
            ],
            compiler_params=pltpu.CompilerParams(
                collective_id=0, has_side_effects=True, vmem_limit_bytes=56 * 1024 * 1024
            ),
        )(queries, keys, values, out_grad, out_weight, residues, decay_rates)
    )


def solution(mesh):
    placed = (
        P("chan", "ctx"),
        P("chan", "ctx"),
        P("chan", "ctx"),
        P("ctx", "chan"),
        P("chan", None),
        P(None, "chan"),
        P(None, "chan"),
    )
    return jax.shard_map(
        local,
        mesh=mesh,
        in_specs=placed,
        out_specs=(
            P("chan", "ctx"),
            P("chan", "ctx"),
            P("chan", "ctx"),
            P(None, ("chan", "ctx")),
            P(None, ("chan", "ctx")),
        ),
        check_vma=False,
    )
```

time: 120 us -> 76.1 us (0.63)
  Pallas kernels: 15.7 us -> 66.8 us
  blocking collectives: 39.6 us -> 0 us
  waiting for transfers between devices: 21.7 us -> 0 us
  matrix products: 16.5 us -> 0 us
  between operations: 14.1 us -> 0.64 us
  starting transfers between devices: 5.21 us -> 0 us
  local copies, waits for them, and re-layouts: 4.01 us -> 8.25 us
  other arithmetic: 2.69 us -> 0 us
    pallas_call x2 -> x1, Pallas kernels: 15.7 us -> 66.8 us  [local(): pl.pallas_call(functools.partial(body, chan_size, ctx_size), out_shape=(g...]
    all_to_all x3 -> x0, blocking collectives: 39.6 us -> none  [the longest x1 13.3 us: local(): lax.all_to_all(elementwise(mixer_grad, queries).T, 'ctx', split_axis=1, c...]
    dot_general x1 -> x0, matrix products: 16.5 us -> none  [local(): jnp.einsum('cd,td->ct', out_weight, gathered, preferred_element_type=jnp....]
    all_gather x1 -> x0, waiting for transfers between devices: 12.6 us -> none  [local(): gathered = lax.all_gather(out_grad, 'chan', axis=1, tiled=True)]
    all_to_all x1 -> x0, waiting for transfers between devices: 8.41 us -> none  [local(): lax.all_to_all(elementwise(keys, values).T, 'ctx', split_axis=1, concat_a...]
    unnamed x6 -> x5, local copies, waits for them, and re-layouts: 0.8 us -> 8.25 us
    all_to_all x1 -> x0, starting transfers between devices: 5.17 us -> none  [local(): lax.all_to_all(elementwise(keys, values).T, 'ctx', split_axis=1, concat_a...]
    convert_element_type x4 -> x0, other arithmetic: 2.69 us -> none  [the longest x2 2.51 us: elementwise(): (left.astype(jnp.float32) * right.astype(jnp.float32)).astype(jnp.bfloat16)]
  transfers between devices with their start and end apart: 2 -> 0, of which waited for: 2 -> 0; matrix products, arithmetic and copies ran while one was open for 3% -> 0% of each run, Pallas kernels for 5% -> 0%
where the time goes in v2:
time: 76.1 us; the launch traced here: 75.7 us
  Pallas kernels  66.8 us (88%)
  local copies, waits for them, and re-layouts  8.25 us (11%)
    pallas_call x1, Pallas kernels, local(): pl.pallas_call(functools.partial(body, chan_size, ctx_size), out_shape=(g...  66.8 us
    unnamed x5, local copies, waits for them, and re-layouts  8.25 us

profile of v2, /device:TPU:0, one launch (start us, length us, event | category | flops | bytes accessed | tf_op | source)
XLA Modules:
  0.0 75.7 jit_solution(3941633265792944185)
XLA Ops:
  0.6 66.8 %shard_map.110 = (bf16[2048,128]{1,0:T(8,128)(2,1)}, bf16[2048,128]{1,0:T(8,128)(2,1)}, bf16[2048,128]{1,0:T(8,128)(2,1)}, f32[16,256]{1,0:T(8,128)}, f32[16,256]{1,0:T(8,128)}) custom-call(bf16[2048,128]{1,0:T(8,128)(2,1)} %queries.1, bf16[2048,128]{1,0:T(8,128)(2,1)} %keys.1, bf16[2048,128]{1,0:T(8,128)(2,1)} %values.1, bf16[128,2048]{1,0:T(8,128)(2,1)} %out_grad.1, ...), custom_call_target="tpu_custom_call" | custom-call | tf_op jit(solution)/shard_map/pallas_call | solution.py:396
  67.4 1.9 %copy.17 = bf16[2048,128]{1,0:T(8,128)(2,1)} copy(bf16[2048,128]{1,0:T(8,128)(2,1)} %get-tuple-element.10) | data formatting | bytes 1048576
  69.3 1.9 %copy.18 = bf16[2048,128]{1,0:T(8,128)(2,1)} copy(bf16[2048,128]{1,0:T(8,128)(2,1)} %get-tuple-element.11) | data formatting | bytes 1048576
  71.1 1.9 %copy.19 = bf16[2048,128]{1,0:T(8,128)(2,1)} copy(bf16[2048,128]{1,0:T(8,128)(2,1)} %get-tuple-element.12) | data formatting | bytes 1048576
  73.0 1.3 %copy.20 = f32[16,256]{1,0:T(8,128)} copy(f32[16,256]{1,0:T(8,128)} %get-tuple-element.13) | data formatting | bytes 32768
  74.3 1.3 %copy.21 = f32[16,256]{1,0:T(8,128)} copy(f32[16,256]{1,0:T(8,128)} %get-tuple-element.14) | data formatting | bytes 32768

commit v3 on v2

--- a/solution.py
+++ b/solution.py
@@ -8,6 +8,7 @@
 from jax.sharding import PartitionSpec as P
 
 STEP = 16
+PIECES = 4
 
 
 def halves(width):
@@ -33,6 +34,10 @@
     return jnp.where(low1, a, pltpu.roll(b, 1, 0)) + jnp.where(low1, pltpu.roll(a, 7, 0), b)
 
 
+def elementwise(left, right):
+    return (left.astype(jnp.float32) * right.astype(jnp.float32)).astype(jnp.bfloat16)
+
+
 def axis_device(axis, index):
     return {axis: index}
 
@@ -69,11 +74,13 @@
     out_weight,
     residues,
     decay_rates,
-    query_grad,
-    key_grad,
-    value_grad,
-    resid_grad,
-    decay_grad,
+    mixer_out,
+    conv_out,
+    product_grad,
+    plain_out,
+    plain_scale,
+    slope_out,
+    slope_scale,
     weight,
     gathered,
     mixer,
@@ -96,6 +103,7 @@
     me = lax.axis_index("ctx")
     channels, tokens = queries.shape
     depth = out_grad.shape[1]
+    piece = depth // PIECES
     width = channels // ctx_size
     order = residues.shape[0]
     columns = halves(width)
@@ -133,12 +141,12 @@
             weight_sems.at[shard],
         )
 
-    def shard_copy(source, shard, going_up):
+    def shard_copy(shard, part, going_up, own=False):
         return pltpu.make_async_remote_copy(
-            src_ref=source,
-            dst_ref=gathered.at[shard],
-            send_sem=(up_sends if going_up else down_sends).at[shard],
-            recv_sem=shard_arrivals.at[shard],
+            src_ref=out_grad.at[:, pl.ds(part * piece, piece)] if own else gathered.at[shard, part],
+            dst_ref=gathered.at[shard, part],
+            send_sem=(up_sends if going_up else down_sends).at[shard, part],
+            recv_sem=shard_arrivals.at[shard, part],
             device_id=axis_device("chan", place + 1 if going_up else place - 1),
             device_id_type=pl.DeviceIdType.MESH,
         )
@@ -171,13 +179,15 @@
         )
     pl.semaphore_wait(barrier, ctx_size + chan_size - 2)
 
-    @pl.when(place < chan_size - 1)
-    def _():
-        shard_copy(out_grad, place, True).start()
-
-    @pl.when(place > 0)
-    def _():
-        shard_copy(out_grad, place, False).start()
+    for part in range(PIECES):
+
+        @pl.when(place < chan_size - 1)
+        def _():
+            shard_copy(place, part, True, True).start()
+
+        @pl.when(place > 0)
+        def _():
+            shard_copy(place, part, False, True).start()
 
     @pl.loop(0, ctx_size)
     def _(step):
@@ -189,12 +199,12 @@
 
     tile = min(channels, 512)
 
-    def multiply(source, shard, first):
+    def multiply(source, shard, taken, first):
         @pl.loop(0, channels // tile)
         def _(index):
             rows = pl.ds(pl.multiple_of(index * tile, tile), tile)
             term = lax.dot_general(
-                weight[shard, rows, :],
+                weight[shard, rows, taken],
                 source[...],
                 (((1,), (1,)), ((), ())),
                 preferred_element_type=f32,
@@ -202,29 +212,32 @@
             mixer[rows, :] = term if first else mixer[rows, :] + term
 
     weight_copy(place).wait()
-    multiply(out_grad, place, True)
+    multiply(out_grad, place, slice(None), True)
 
     def gather_step(distance):
         sides = (
             (place - distance, place >= distance, place < chan_size - 1, True),
             (place + distance, place + distance < chan_size, place > 0, False),
         )
-        for shard, present, onward, going_up in sides:
-
-            @pl.when(present)
-            def _():
-                shard_copy(gathered.at[shard], shard, going_up).wait_recv()
-
-                @pl.when(onward)
+        for part in range(PIECES):
+            for shard, present, onward, going_up in sides:
+
+                @pl.when(present)
                 def _():
-                    shard_copy(gathered.at[shard], shard, going_up).start()
-
-        for shard, present, onward, going_up in sides:
-
-            @pl.when(present)
-            def _():
-                weight_copy(shard).wait()
-                multiply(gathered.at[shard], shard, False)
+                    shard_copy(shard, part, going_up).wait_recv()
+
+                    @pl.when(onward)
+                    def _():
+                        shard_copy(shard, part, going_up).start()
+
+            for shard, present, onward, going_up in sides:
+
+                @pl.when(present)
+                def _():
+                    if part == 0:
+                        weight_copy(shard).wait()
+                    taken = pl.ds(part * piece, piece)
+                    multiply(gathered.at[shard, part], shard, taken, False)
 
     def mode_groups(start, lanes):
         groups = []
@@ -322,8 +335,10 @@
                 root = jnp.sqrt(2.0 * rate)
                 plain_sum, moment_sum = final[position][g][2:]
                 put = (pl.ds(8 * g, 8), pl.ds(start, lanes))
-                resid_grad[put] = root * plain_sum
-                decay_grad[put] = amplitude * root * (0.5 * plain_sum - rate * moment_sum)
+                plain_out[put] = plain_sum
+                plain_scale[put] = root
+                slope_out[put] = 0.5 * plain_sum - rate * moment_sum
+                slope_scale[put] = amplitude * root
 
     for distance in range(1, chan_size):
         gather_step(distance)
@@ -336,7 +351,9 @@
     def _(step):
         other = lax.rem(me + 1 + step, ctx_size)
         rows = pl.ds(pl.multiple_of(other * width, width), width)
-        pair = mixer[rows, :].astype(bf16).astype(f32) * queries[rows, :].astype(f32)
+        rounded = mixer[rows, :].astype(bf16)
+        mixer_out[rows, :] = rounded
+        pair = rounded.astype(f32) * queries[rows, :].astype(f32)
         conv_grad_out[other] = pair.astype(bf16).astype(f32).T.astype(bf16)
         send_or_keep(conv_grad_links, other)
 
@@ -346,16 +363,13 @@
     def _(slot):
         await_slot(conv_out_links, slot)
         rows = pl.ds(pl.multiple_of(slot * width, width), width)
-        result = conv_out_in[slot].astype(f32).T
-        query_grad[rows, :] = (mixer[rows, :].astype(bf16).astype(f32) * result).astype(bf16)
+        conv_out[rows, :] = conv_out_in[slot].astype(f32).T.astype(bf16)
 
     @pl.loop(0, ctx_size)
     def _(slot):
         await_slot(product_grad_links, slot)
         rows = pl.ds(pl.multiple_of(slot * width, width), width)
-        result = product_grad_in[slot].astype(f32).T
-        key_grad[rows, :] = (result * values[rows, :].astype(f32)).astype(bf16)
-        value_grad[rows, :] = (result * keys[rows, :].astype(f32)).astype(bf16)
+        product_grad[rows, :] = product_grad_in[slot].astype(f32).T.astype(bf16)
 
     @pl.loop(0, ctx_size)
     def _(other):
@@ -372,8 +386,8 @@
 
             @pl.when(present & onward)
             def _():
-                source = out_grad if distance == 0 else gathered.at[shard]
-                shard_copy(source, shard, going_up).wait_send()
+                for part in range(PIECES):
+                    shard_copy(shard, part, going_up, distance == 0).wait_send()
 
 
 def local(queries, keys, values, out_grad, out_weight, residues, decay_rates):
@@ -392,28 +406,33 @@
     vmem = pl.BlockSpec(memory_space=pltpu.VMEM)
     slots = pltpu.VMEM((ctx_size, tokens, width), jnp.bfloat16)
     dma = pltpu.SemaphoreType.DMA
-    return tuple(
-        pl.pallas_call(
+    mixer, conv_out, product_grad, plain, plain_scale, slope, slope_scale = pl.pallas_call(
             functools.partial(body, chan_size, ctx_size),
-            out_shape=(gate, gate, gate, grads, grads),
+            out_shape=(gate,) * 3 + (grads,) * 4,
             in_specs=[vmem, vmem, vmem, vmem, pl.BlockSpec(memory_space=pl.ANY), vmem, vmem],
-            out_specs=(vmem,) * 5,
+            out_specs=(vmem,) * 7,
             scratch_shapes=[
                 pltpu.VMEM((chan_size, channels, depth), jnp.bfloat16),
-                pltpu.VMEM((chan_size, tokens, depth), jnp.bfloat16),
+                pltpu.VMEM((chan_size, PIECES, tokens, depth // PIECES), jnp.bfloat16),
                 pltpu.VMEM((channels, tokens), jnp.float32),
                 *[slots] * 8,
                 dma((chan_size,)),
-                dma((chan_size,)),
-                dma((chan_size,)),
-                dma((chan_size,)),
+                dma((chan_size, PIECES)),
+                dma((chan_size, PIECES)),
+                dma((chan_size, PIECES)),
                 dma((4, ctx_size)),
                 dma((4, ctx_size)),
             ],
             compiler_params=pltpu.CompilerParams(
                 collective_id=0, has_side_effects=True, vmem_limit_bytes=56 * 1024 * 1024
             ),
-        )(queries, keys, values, out_grad, out_weight, residues, decay_rates)
+    )(queries, keys, values, out_grad, out_weight, residues, decay_rates)
+    return (
+        elementwise(mixer, conv_out),
+        elementwise(product_grad, values),
+        elementwise(product_grad, keys),
+        plain_scale * plain,
+        slope_scale * slope,
     )
 
 

time: 76.1 us -> 70.5 us (0.926)
  local copies, waits for them, and re-layouts: 8.25 us -> 0.01 us
  other arithmetic: 0 us -> 5.5 us
  Pallas kernels: 66.8 us -> 63.9 us
    unnamed x5 -> x4, local copies, waits for them, and re-layouts: 8.25 us -> 0.01 us
    pallas_call x1, Pallas kernels: 66.8 us -> 63.9 us  [local(): pl.pallas_call(functools.partial(body, chan_size, ctx_size), out_shape=(g...]
    convert_element_type x0 -> x1, other arithmetic: none -> 2.81 us  [elementwise(): (left.astype(jnp.float32) * right.astype(jnp.float32)).astype(jnp.bfloat16)]
    mul x0 -> x2, other arithmetic: none -> 2.69 us  [the longest x1 1.34 us: local(): plain_scale * plain]
where the time goes in v3:
time: 70.5 us; the launch traced here: 70.1 us
  Pallas kernels  63.9 us (91%)
  other arithmetic  5.5 us (8%)
    pallas_call x1, Pallas kernels, local(): pl.pallas_call(functools.partial(body, chan_size, ctx_size), out_shape=(g...  63.9 us
    convert_element_type x1, other arithmetic, elementwise(): (left.astype(jnp.float32) * right.astype(jnp.float32)).astype(jnp.bfloat16)  2.81 us

profile of v3, /device:TPU:0, one launch (start us, length us, event | category | flops | bytes accessed | tf_op | source)
XLA Modules:
  0.0 70.1 jit_solution(9538502634879726747)
XLA Ops:
  0.6 0.0 copy-start.1
  0.6 0.0 copy-start
  0.7 63.9 %shard_map.110 = (bf16[2048,128]{1,0:T(8,128)(2,1)}, bf16[2048,128]{1,0:T(8,128)(2,1)}, bf16[2048,128]{1,0:T(8,128)(2,1)}, f32[16,256]{1,0:T(8,128)}, f32[16,256...) custom-call(bf16[2048,128]{1,0:T(8,128)(2,1)} %queries.1, bf16[2048,128]{1,0:T(8,128)(2,1)} %keys.1, ...), custom_call_target="tpu_custom_call" | custom-call | tf_op jit(solution)/shard_map/pallas_call | solution.py:409
  64.6 0.0 copy-done.1
  64.6 0.0 copy-done
  64.6 2.8 %fusion.1 = (bf16[2048,128]{1,0:T(8,128)(2,1)}, bf16[2048,128]{1,0:T(8,128)(2,1)}, bf16[2048,128]{1,0:T(8,128)(2,1)}) fusion(bf16[2048,128]{1,0:T(8,128)(2,1)} %get-tuple-element.14, bf16[2048,128]{1,0:T(8,128)(2,1)S(1)} %copy-done, bf16[2048,128]{1,0:T(8,128)(2,1)S(1)} %copy-done.1, bf16[2048,128]{1,0:T(8,128)(2,1)} %get-tuple-element.13, ...), kind=kLoop, calls=%fused_computation.3 | loop fusion | flops 2883584 | bytes 4194304 | tf_op jit(solution)/shard_map/convert_element_type | solution.py:38
  67.4 1.3 %mul.18 = f32[16,256]{1,0:T(8,128)} multiply(f32[16,256]{1,0:T(8,128)} %get-tuple-element.15, f32[16,256]{1,0:T(8,128)} %get-tuple-element.16) | non-fusion elementwise | flops 4096 | bytes 49152 | tf_op jit(solution)/shard_map/mul | solution.py:434
  68.7 1.3 %mul.19 = f32[16,256]{1,0:T(8,128)} multiply(f32[16,256]{1,0:T(8,128)} %get-tuple-element.17, f32[16,256]{1,0:T(8,128)} %get-tuple-element.18) | non-fusion elementwise | flops 4096 | bytes 49152 | tf_op jit(solution)/shard_map/mul | solution.py:435
Async XLA Ops:
  0.6 63.9 %copy-start.1 = (bf16[2048,128]{1,0:T(8,128)(2,1)S(1)}, bf16[2048,128]{1,0:T(8,128)(2,1)}, u32[]{:S(2)}) copy-start(bf16[2048,128]{1,0:T(8,128)(2,1)} %values.1) | copy-start | bytes 1572868
  0.6 63.9 %copy-start = (bf16[2048,128]{1,0:T(8,128)(2,1)S(1)}, bf16[2048,128]{1,0:T(8,128)(2,1)}, u32[]{:S(2)}) copy-start(bf16[2048,128]{1,0:T(8,128)(2,1)} %keys.1) | copy-start | bytes 1572868
